TPU v7x, 256 devices: a whole 4x4x8 slice. The times are simulated.
256 devices in a mesh: mp: 2 (over x_hi), row: 8 (over z), col: 16 (over x_lo, y, core).
Axes of the slice: x: 4 (x_hi: 2, x_lo: 2; x = x_hi * 2 + x_lo), y: 4, z: 8, core: 2. Of those that a mesh axis runs over, the one named last changes fastest.
Arguments:
- gram_tiles: bfloat16 [4, 16, 8, 128, 16384], P('mp', None, 'row', None, 'col'), may hold values from -4 to 64, as said below
- weights: bfloat16 [4, 16384, 128], P('mp', ('col', 'row')), may hold values from -8 to 8
- damping: float32 [128], replicated, may hold values from 0.5 to 4
Outputs:
- merged: float32 [16384, 128], P(('col', 'row'))
- residual: float32 [16384, 128], P(('col', 'row'))
Inputs may be any that keep to these rules, and one draw needn't show every extreme that they name: `gram_tiles`: each model's 16384 x 16384 Gram, read as in the first step, is symmetric positive definite.
All inputs are finite; a program needn't handle non-finite values.
Results may differ from a plain program's by a relative error of at most 0.012.
The roundings to bfloat16 on the way count: a program that leaves them out, or rounds other values in their place, can miss the bound.
Values may be sent and summed in bfloat16 or wider, within the bound.
No kernel may reach another device: no remote copies, remote signals or barrier semaphores. Data moves between devices by JAX's collectives and lax.ppermute only.
A program may use at most 64 MiB of HBM per device.

v0:
```python
import jax
import jax.numpy as jnp
from jax import lax
from jax.sharding import PartitionSpec as P

ITERS = 2


def contract_rows(gram_tile, portion):
    spread = jnp.broadcast_to(portion, (gram_tile.shape[0],) + portion.shape[1:])
    return jnp.einsum("mij,mjk->ik", gram_tile, spread, preferred_element_type=jnp.float32)


def apply_models(gram_tile, vectors):
    partial_value = contract_rows(gram_tile, lax.all_gather(vectors, "row", axis=1, tiled=True))
    summed = lax.psum_scatter(partial_value, "col", scatter_dimension=0, tiled=True)
    return (lax.psum(summed, "mp"), partial_value)


def squares(residual):
    return lax.psum(jnp.sum(residual * residual, axis=0), ("row", "col"))


def on_device(gram_tiles, weights, damping):
    shape_in = gram_tiles.shape
    gram_tile = gram_tiles.reshape(
        shape_in[0], shape_in[1] * shape_in[2] * shape_in[3], shape_in[4]
    )
    target, unused = apply_models(gram_tile, weights)
    merged = jnp.zeros_like(target)
    residual = target
    direction = target
    norm_now = squares(residual)
    for iteration in range(ITERS):
        low_dir = direction.astype(jnp.bfloat16)
        applied, partial_value = apply_models(gram_tile, low_dir[None])
        dir_wide = low_dir.astype(jnp.float32)
        applied = applied + damping[None, :] * dir_wide
        curve_term = lax.psum(jnp.sum(dir_wide * applied, axis=0), ("row", "col"))
        step_size = norm_now / curve_term
        merged = merged + step_size[None, :] * direction
        residual = residual - step_size[None, :] * applied
        if iteration + 1 < ITERS:
            norm_next = squares(residual)
            direction = residual + (norm_next / norm_now)[None, :] * direction
            norm_now = norm_next
    return (merged, residual)


def solution(mesh):
    in_specs = (P("mp", None, "row", None, "col"), P("mp", ("col", "row"), None), P())
    out_specs = (P(("col", "row"), None), P(("col", "row"), None))
    return jax.shard_map(
        on_device, mesh=mesh, in_specs=in_specs, out_specs=out_specs, check_vma=False
    )
```

profile of v0, /device:TPU:4, one launch (start us, length us, event | category | flops | bytes accessed | tf_op | source)
XLA Modules:
  0.0 1248.6 jit_solution(5157626509282699537)
XLA Ops:
  7.2 29.3 %all_gather.9 = bf16[2,1024,128]{2,1,0:T(8,128)(2,1)S(1)} all-gather(bf16[2,128,128]{2,1,0:T(8,128)(2,1)} %param.4), channel_id=1, replica_groups=mesh['mp'=2,'row'=8,'col'=16] {'row'}, dimensions={1}, use_global_device_ids=true | all-gather | bytes 589824 | tf_op jit(solution)/shard_map/all_gather | solution.py:15
  36.5 6.7 convolution_bitcast_fusion.2
  43.3 63.9 %reduce-scatter.4.cloned.1.call-done = f32[128,128]{1,0:T(8,128)} async-done(((f32[2048,128]{1,0:T(8,128)}), f32[128,128]{1,0:T(8,128)}) %reduce-scatter.4.cloned.1.call-update) | async-done | bytes 65552 | tf_op jit(solution)/shard_map/reduce_scatter | solution.py:16
  107.3 33.3 %all-reduce.5.cloned.1.call-done = f32[128,128]{1,0:T(8,128)} async-done(((f32[128,128]{1,0:T(8,128)}), f32[128,128]{1,0:T(8,128)}) %all-reduce.5.cloned.1.call-update) | async-done | bytes 65552 | tf_op jit(solution)/shard_map/psum | solution.py:17
  140.6 0.9 convert_element_type.12
  141.5 26.0 %all-gather = bf16[1024,128]{1,0:T(8,128)(2,1)S(1)} all-gather(bf16[128,128]{1,0:T(8,128)(2,1)S(1)} %convert_element_type.12), channel_id=2, replica_groups=mesh['mp'=2,'row'=8,'col'=16] {'row'}, dimensions={0}, use_global_device_ids=true | all-gather | bytes 294912 | tf_op jit(solution)/shard_map/all_gather | solution.py:15
  167.6 0.1 copy.5
  167.7 6.7 convolution_bitcast_fusion.1
  174.5 65.0 %reduce-scatter.6.cloned.1.call-done = f32[128,128]{1,0:T(8,128)} async-done(((f32[2048,128]{1,0:T(8,128)}), f32[128,128]{1,0:T(8,128)}) %reduce-scatter.6.cloned.1.call-update) | async-done | bytes 65552 | tf_op jit(solution)/shard_map/reduce_scatter | solution.py:16
  239.6 33.3 %all-reduce.7.cloned.1.call-done = f32[128,128]{1,0:T(8,128)} async-done(((f32[128,128]{1,0:T(8,128)}), f32[128,128]{1,0:T(8,128)}) %all-reduce.7.cloned.1.call-update) | async-done | bytes 65552 | tf_op jit(solution)/shard_map/psum | solution.py:17
  272.9 0.9 fusion.3
  273.8 281.3 %all-reduce = (f32[128]{0:T(128)S(1)}, f32[128]{0:T(128)S(1)}) all-reduce(f32[128]{0:T(128)S(1)} %get-tuple-element.3, f32[128]{0:T(128)S(1)} %get-tuple-element.2), channel_id=1, replica_groups=mesh['mp'=2,'row'=8,'col'=16] {'row','col'}, use_global_device_ids=true, to_apply=%region_3.0 | all-reduce | flops 256 | bytes 2048 | tf_op jit(solution)/shard_map/psum | solution.py:21
  555.1 0.9 multiply_reduce_fusion
  556.0 275.6 %psum.53 = f32[128]{0:T(128)S(1)} all-reduce(f32[128]{0:T(128)S(1)} %multiply_reduce_fusion), channel_id=1, replica_groups=mesh['mp'=2,'row'=8,'col'=16] {'row','col'}, use_global_device_ids=true, to_apply=%region_9.0 | all-reduce | flops 128 | bytes 1024 | tf_op jit(solution)/shard_map/psum | solution.py:21
  831.6 0.9 fusion.6
  832.4 24.9 %all-gather.1 = bf16[1024,128]{1,0:T(8,128)(2,1)S(1)} all-gather(bf16[128,128]{1,0:T(8,128)(2,1)S(1)} %fusion.6), channel_id=3, replica_groups=mesh['mp'=2,'row'=8,'col'=16] {'row'}, dimensions={0}, use_global_device_ids=true | all-gather | bytes 294912 | tf_op jit(solution)/shard_map/all_gather | solution.py:15
  857.3 0.1 copy.7
  857.5 6.7 convolution_bitcast_fusion
  864.2 0.0 all-reduce.9.cloned.1.call-start
  864.3 60.5 %reduce-scatter.8.cloned.1.call-done = f32[128,128]{1,0:T(8,128)} async-done(((f32[2048,128]{1,0:T(8,128)}), f32[128,128]{1,0:T(8,128)}) %reduce-scatter.8.cloned.1.call-update) | async-done | bytes 65552 | tf_op jit(solution)/shard_map/reduce_scatter | solution.py:16
  924.8 33.2 %all-reduce.9.cloned.1.call-done = f32[128,128]{1,0:T(8,128)} async-done(((f32[128,128]{1,0:T(8,128)}), f32[128,128]{1,0:T(8,128)}) %all-reduce.9.cloned.1.call-update) | async-done | bytes 65552 | tf_op jit(solution)/shard_map/psum | solution.py:17
  958.1 0.9 fusion.5
  958.9 281.3 %psum.55 = f32[128]{0:T(128)S(1)} all-reduce(f32[128]{0:T(128)S(1)} %fusion.5), channel_id=1, replica_groups=mesh['mp'=2,'row'=8,'col'=16] {'row','col'}, use_global_device_ids=true, to_apply=%region_13.0 | all-reduce | flops 128 | bytes 1024 | tf_op jit(solution)/shard_map/psum | solution.py:39
  1240.2 1.5 multiply_subtract_fusion
  (20 shorter events, 0.3 us)
Async XLA Ops:
  7.2 100.1 %reduce-scatter.4.cloned.1.call-start = ((), (), s32[]{:S(2)}) async-start(), calls=%async_computation.3 | async-start | bytes 1114112 | tf_op jit(solution)/shard_map/reduce_scatter | solution.py:16
  43.3 229.6 %copy-start.2 = (f32[128]{0:T(128)S(1)}, f32[128]{0:T(128)}, u32[]{:S(2)}) copy-start(f32[128]{0:T(128)} %param.5) | copy-start | bytes 1540
  43.3 97.3 %all-reduce.5.cloned.1.call-start = ((), (), s32[]{:S(2)}) async-start(), calls=%async_computation.4 | async-start | bytes 131072 | tf_op jit(solution)/shard_map/psum | solution.py:17
  107.3 132.3 %reduce-scatter.6.cloned.1.call-start = ((), (), s32[]{:S(2)}) async-start(), calls=%async_computation.5 | async-start | bytes 1114112 | tf_op jit(solution)/shard_map/reduce_scatter | solution.py:16
  140.6 132.3 %copy-start = (f32[128,128]{1,0:T(8,128)S(1)}, f32[128,128]{1,0:T(8,128)}, u32[]{:S(2)}) copy-start(f32[128,128]{1,0:T(8,128)} %all-reduce.5.cloned.1.call-done) | copy-start | bytes 196612
  174.5 98.5 %all-reduce.7.cloned.1.call-start = ((), (), s32[]{:S(2)}) async-start(), calls=%async_computation.6 | async-start | bytes 131072 | tf_op jit(solution)/shard_map/psum | solution.py:17
  239.6 685.2 %reduce-scatter.8.cloned.1.call-start = ((), (), s32[]{:S(2)}) async-start(), calls=%async_computation.7 | async-start | bytes 1114112 | tf_op jit(solution)/shard_map/reduce_scatter | solution.py:16
  273.8 966.4 %copy-start.1 = (f32[128,128]{1,0:T(8,128)S(1)}, f32[128,128]{1,0:T(8,128)}, u32[]{:S(2)}) copy-start(f32[128,128]{1,0:T(8,128)} %all-reduce.7.cloned.1.call-done) | copy-start | bytes 196612
  864.2 93.9 %all-reduce.9.cloned.1.call-start = ((), (), s32[]{:S(2)}) async-start(), calls=%async_computation.8 | async-start | bytes 131072 | tf_op jit(solution)/shard_map/psum | solution.py:17
Sparse Core Ops, SparseCore 0:
  43.4 63.7 reduce-scatter.3
  109.8 30.8 all-reduce.4
  174.6 64.9 reduce-scatter.5
  242.0 30.9 all-reduce.6
  864.3 60.4 reduce-scatter.7
  927.2 30.8 all-reduce.8
where the time goes:
time: 1250 us
  blocking collectives  918 us (73%)
  waiting for transfers between devices  289 us (23%)
  matrix products  20.2 us (2%)
  between operations  14.1 us (1%)
    psum x2, blocking collectives, squares(): return lax.psum(jnp.sum(residual * residual, axis=0), ('row', 'col'))  557 us
    psum x1, blocking collectives, on_device(): curve_term = lax.psum(jnp.sum(dir_wide * applied, axis=0), ('row', 'col'))  281 us
    reduce_scatter x3, waiting for transfers between devices, apply_models(): lax.psum_scatter(partial_value, 'col', scatter_dimension=0, tiled=True)  189 us
    psum x3, waiting for transfers between devices, apply_models(): return (lax.psum(summed, 'mp'), partial_value)  99.9 us
    all_gather x3, blocking collectives, apply_models(): lax.all_gather(vectors, 'row', axis=1, tiled=True)  80.2 us
  transfers between devices with their start and end apart: 6, of which 6 were waited for; matrix products, arithmetic and copies ran while one was open for 0% of the time, Pallas kernels for 0%

commit v1 on v0

--- a/solution.py
+++ b/solution.py
@@ -36,7 +36,7 @@
         applied, partial_value = apply_models(gram_tile, low_dir[None])
         dir_wide = low_dir.astype(jnp.float32)
         applied = applied + damping[None, :] * dir_wide
-        curve_term = lax.psum(jnp.sum(dir_wide * applied, axis=0), ("row", "col"))
+        curve_term = lax.psum(lax.psum(jnp.sum(dir_wide * applied, axis=0), "col"), "row")
         step_size = norm_now / curve_term
         merged = merged + step_size[None, :] * direction
         residual = residual - step_size[None, :] * applied

time: 1250 us -> 1060 us (0.85)
  blocking collectives: 918 us -> 726 us
    psum x1 -> x4, blocking collectives: 281 us -> 95.1 us  [the longest x2 60.2 us: on_device(): lax.psum(jnp.sum(dir_wide * applied, axis=0), 'col')]
where the time goes in v1:
time: 1060 us
  blocking collectives  726 us (68%)
  waiting for transfers between devices  290 us (27%)
  matrix products  20.2 us (2%)
  between operations  14.1 us (1%)
    psum x2, blocking collectives, squares(): return lax.psum(jnp.sum(residual * residual, axis=0), ('row', 'col'))  551 us
    reduce_scatter x3, waiting for transfers between devices, apply_models(): lax.psum_scatter(partial_value, 'col', scatter_dimension=0, tiled=True)  190 us
    psum x3, waiting for transfers between devices, apply_models(): return (lax.psum(summed, 'mp'), partial_value)  99.9 us
    all_gather x3, blocking collectives, apply_models(): lax.all_gather(vectors, 'row', axis=1, tiled=True)  80.2 us
    psum x2, blocking collectives, on_device(): lax.psum(jnp.sum(dir_wide * applied, axis=0), 'col')  60.2 us
    psum x2, blocking collectives, on_device(): lax.psum(lax.psum(jnp.sum(dir_wide * applied, axis=0), 'col'), 'row')  34.9 us
  transfers between devices with their start and end apart: 6, of which 6 were waited for; matrix products, arithmetic and copies ran while one was open for 0% of the time, Pallas kernels for 0%

profile of v1, /device:TPU:4, one launch (start us, length us, event | category | flops | bytes accessed | tf_op | source)
XLA Modules:
  0.0 1056.9 jit_solution(3575240076810573809)
XLA Ops:
  7.2 29.3 %all_gather.9 = bf16[2,1024,128]{2,1,0:T(8,128)(2,1)S(1)} all-gather(bf16[2,128,128]{2,1,0:T(8,128)(2,1)} %param.4), channel_id=1, replica_groups=mesh['mp'=2,'row'=8,'col'=16] {'row'}, dimensions={1}, use_global_device_ids=true | all-gather | bytes 589824 | tf_op jit(solution)/shard_map/all_gather | solution.py:15
  36.5 6.7 convolution_bitcast_fusion.2
  43.3 63.9 %reduce-scatter.4.cloned.1.call-done = f32[128,128]{1,0:T(8,128)} async-done(((f32[2048,128]{1,0:T(8,128)}), f32[128,128]{1,0:T(8,128)}) %reduce-scatter.4.cloned.1.call-update) | async-done | bytes 65552 | tf_op jit(solution)/shard_map/reduce_scatter | solution.py:16
  107.3 33.3 %all-reduce.4.cloned.1.call-done = f32[128,128]{1,0:T(8,128)} async-done(((f32[128,128]{1,0:T(8,128)}), f32[128,128]{1,0:T(8,128)}) %all-reduce.4.cloned.1.call-update) | async-done | bytes 65552 | tf_op jit(solution)/shard_map/psum | solution.py:17
  140.6 0.9 convert_element_type.12
  141.5 26.0 %all-gather = bf16[1024,128]{1,0:T(8,128)(2,1)S(1)} all-gather(bf16[128,128]{1,0:T(8,128)(2,1)S(1)} %convert_element_type.12), channel_id=2, replica_groups=mesh['mp'=2,'row'=8,'col'=16] {'row'}, dimensions={0}, use_global_device_ids=true | all-gather | bytes 294912 | tf_op jit(solution)/shard_map/all_gather | solution.py:15
  167.7 6.7 convolution_bitcast_fusion.1
  174.5 65.0 %reduce-scatter.6.cloned.1.call-done = f32[128,128]{1,0:T(8,128)} async-done(((f32[2048,128]{1,0:T(8,128)}), f32[128,128]{1,0:T(8,128)}) %reduce-scatter.6.cloned.1.call-update) | async-done | bytes 65552 | tf_op jit(solution)/shard_map/reduce_scatter | solution.py:16
  239.6 33.3 %all-reduce.6.cloned.1.call-done = f32[128,128]{1,0:T(8,128)} async-done(((f32[128,128]{1,0:T(8,128)}), f32[128,128]{1,0:T(8,128)}) %all-reduce.6.cloned.1.call-update) | async-done | bytes 65552 | tf_op jit(solution)/shard_map/psum | solution.py:17
  272.9 0.9 fusion.3
  273.8 30.1 %psum.66 = f32[128]{0:T(128)S(1)} all-reduce(f32[128]{0:T(128)S(1)} %get-tuple-element.2), channel_id=1, replica_groups=mesh['mp'=2,'row'=8,'col'=16] {'col'}, use_global_device_ids=true, to_apply=%region_7.0 | all-reduce | flops 128 | bytes 1024 | tf_op jit(solution)/shard_map/psum | solution.py:39
  303.9 17.5 %psum.67 = f32[128]{0:T(128)S(1)} all-reduce(f32[128]{0:T(128)S(1)} %psum.66), channel_id=1, replica_groups=mesh['mp'=2,'row'=8,'col'=16] {'row'}, use_global_device_ids=true, to_apply=%region_8.0 | all-reduce | flops 128 | bytes 1024 | tf_op jit(solution)/shard_map/psum | solution.py:39
  321.4 275.6 %psum.64 = f32[128]{0:T(128)S(1)} all-reduce(f32[128]{0:T(128)S(1)} %get-tuple-element.3), channel_id=1, replica_groups=mesh['mp'=2,'row'=8,'col'=16] {'row','col'}, use_global_device_ids=true, to_apply=%region_3.0 | all-reduce | flops 128 | bytes 1024 | tf_op jit(solution)/shard_map/psum | solution.py:21
  597.0 0.9 multiply_reduce_fusion
  597.8 275.6 %psum.68 = f32[128]{0:T(128)S(1)} all-reduce(f32[128]{0:T(128)S(1)} %multiply_reduce_fusion), channel_id=1, replica_groups=mesh['mp'=2,'row'=8,'col'=16] {'row','col'}, use_global_device_ids=true, to_apply=%region_10.0 | all-reduce | flops 128 | bytes 1024 | tf_op jit(solution)/shard_map/psum | solution.py:21
  873.4 0.9 fusion.6
  874.3 24.9 %all-gather.1 = bf16[1024,128]{1,0:T(8,128)(2,1)S(1)} all-gather(bf16[128,128]{1,0:T(8,128)(2,1)S(1)} %fusion.6), channel_id=3, replica_groups=mesh['mp'=2,'row'=8,'col'=16] {'row'}, dimensions={0}, use_global_device_ids=true | all-gather | bytes 294912 | tf_op jit(solution)/shard_map/all_gather | solution.py:15
  899.3 6.7 convolution_bitcast_fusion
  906.1 60.7 %reduce-scatter.8.cloned.1.call-done = f32[128,128]{1,0:T(8,128)} async-done(((f32[2048,128]{1,0:T(8,128)}), f32[128,128]{1,0:T(8,128)}) %reduce-scatter.8.cloned.1.call-update) | async-done | bytes 65552 | tf_op jit(solution)/shard_map/reduce_scatter | solution.py:16
  966.9 33.2 %all-reduce.8.cloned.1.call-done = f32[128,128]{1,0:T(8,128)} async-done(((f32[128,128]{1,0:T(8,128)}), f32[128,128]{1,0:T(8,128)}) %all-reduce.8.cloned.1.call-update) | async-done | bytes 65552 | tf_op jit(solution)/shard_map/psum | solution.py:17
  1000.1 0.9 fusion.5
  1001.0 30.1 %psum.70 = f32[128]{0:T(128)S(1)} all-reduce(f32[128]{0:T(128)S(1)} %fusion.5), channel_id=1, replica_groups=mesh['mp'=2,'row'=8,'col'=16] {'col'}, use_global_device_ids=true, to_apply=%region_14.0 | all-reduce | flops 128 | bytes 1024 | tf_op jit(solution)/shard_map/psum | solution.py:39
  1031.1 17.5 %psum.71 = f32[128]{0:T(128)S(1)} all-reduce(f32[128]{0:T(128)S(1)} %psum.70), channel_id=1, replica_groups=mesh['mp'=2,'row'=8,'col'=16] {'row'}, use_global_device_ids=true, to_apply=%region_15.0 | all-reduce | flops 128 | bytes 1024 | tf_op jit(solution)/shard_map/psum | solution.py:39
  1048.5 1.5 multiply_subtract_fusion
  (23 shorter events, 0.7 us)
Async XLA Ops:
  7.2 100.1 %reduce-scatter.4.cloned.1.call-start = ((), (), s32[]{:S(2)}) async-start(), calls=%async_computation.3 | async-start | bytes 1114112 | tf_op jit(solution)/shard_map/reduce_scatter | solution.py:16
  43.3 229.6 %copy-start.2 = (f32[128]{0:T(128)S(1)}, f32[128]{0:T(128)}, u32[]{:S(2)}) copy-start(f32[128]{0:T(128)} %param.5) | copy-start | bytes 1540
  43.3 97.3 %all-reduce.4.cloned.1.call-start = ((), (), s32[]{:S(2)}) async-start(), calls=%async_computation.4 | async-start | bytes 131072 | tf_op jit(solution)/shard_map/psum | solution.py:17
  107.3 132.3 %reduce-scatter.6.cloned.1.call-start = ((), (), s32[]{:S(2)}) async-start(), calls=%async_computation.5 | async-start | bytes 1114112 | tf_op jit(solution)/shard_map/reduce_scatter | solution.py:16
  140.6 132.3 %copy-start = (f32[128,128]{1,0:T(8,128)S(1)}, f32[128,128]{1,0:T(8,128)}, u32[]{:S(2)}) copy-start(f32[128,128]{1,0:T(8,128)} %all-reduce.4.cloned.1.call-done) | copy-start | bytes 196612
  174.5 98.5 %all-reduce.6.cloned.1.call-start = ((), (), s32[]{:S(2)}) async-start(), calls=%async_computation.6 | async-start | bytes 131072 | tf_op jit(solution)/shard_map/psum | solution.py:17
  239.6 727.2 %reduce-scatter.8.cloned.1.call-start = ((), (), s32[]{:S(2)}) async-start(), calls=%async_computation.7 | async-start | bytes 1114112 | tf_op jit(solution)/shard_map/reduce_scatter | solution.py:16
  273.8 774.7 %copy-start.1 = (f32[128,128]{1,0:T(8,128)S(1)}, f32[128,128]{1,0:T(8,128)}, u32[]{:S(2)}) copy-start(f32[128,128]{1,0:T(8,128)} %all-reduce.6.cloned.1.call-done) | copy-start | bytes 196612
  906.1 94.0 %all-reduce.8.cloned.1.call-start = ((), (), s32[]{:S(2)}) async-start(), calls=%async_computation.8 | async-start | bytes 131072 | tf_op jit(solution)/shard_map/psum | solution.py:17
Sparse Core Ops, SparseCore 0:
  43.4 63.7 reduce-scatter.3
  109.8 30.8 all-reduce.3
  174.6 64.9 reduce-scatter.5
  242.0 30.9 all-reduce.5
  906.2 60.6 reduce-scatter.7
  969.2 30.8 all-reduce.7
